TPU v7x, 32 devices: a whole 2x2x4 slice. The times are simulated.
32 devices in a mesh: league: 4 (over x, core), env: 8 (over z, y).
Axes of the slice: x: 2, y: 2, z: 4, core: 2. Of those that a mesh axis runs over, the one named last changes fastest.
Arguments:
- obs_own: bfloat16 [4, 2, 128, 16, 2048], P('league', None, 'env'), may hold values from -6 to 6
- obs_opp: bfloat16 [4, 2, 128, 16, 2048], P('league', None, 'env'), may hold values from -6 to 6
- actions: int32 [4, 2, 2, 128, 16], P('league', None, None, 'env'), may hold values from 0 to 255
- opponent_picks: int32 [4, 2], P('league'), may hold values from 0 to 3
- policy_weight: bfloat16 [4, 2048, 2048], P('league', 'env'), may hold values from -0.125 to 0.125
- policy_gain: bfloat16 [4, 2048], P('league'), may hold values from 0.25 to 1.75
- action_table: bfloat16 [256, 2048], replicated, may hold values from -6 to 6
- value_gain: bfloat16 [2048], replicated, may hold values from 0.25 to 1.75
- value_up: bfloat16 [2048, 1024], replicated, may hold values from -0.125 to 0.125
- value_out: bfloat16 [1024], replicated, may hold values from -0.1875 to 0.1875
Outputs:
- learner_rows: bfloat16 [4, 2, 16, 2048, 128], P('league', None, None, 'env')
- values: float32 [4, 2, 128, 16], P('league', None, 'env')
All inputs are finite; a program needn't handle non-finite values.
Results may differ from a plain program's by a relative error of at most 0.0054.
Values may be sent and summed in bfloat16 or wider, within the bound.
A program may use at most 128 MiB of HBM per device.

v0:
```python
import jax
import jax.numpy as jnp
from jax import lax
from jax.sharding import PartitionSpec as P


def rms_norm(inputs, gain):
    scale = lax.rsqrt(jnp.mean(inputs * inputs, axis=-1, keepdims=True) + 1e-05)
    return inputs * scale * gain.astype(jnp.float32)


def local(
    obs_own,
    obs_opp,
    actions,
    opponent_picks,
    policy_weight,
    policy_gain,
    action_table,
    value_gain,
    value_up,
    value_out,
):
    round_count = obs_own.shape[1]
    env_count = obs_own.shape[2]
    step_count = obs_own.shape[3]
    model_width = obs_own.shape[4]
    row_count = env_count * step_count
    weight_shard = policy_weight[0]
    own_gain = policy_gain[0]
    group_count = lax.axis_size("league")
    my_group = lax.axis_index("league")
    own_inputs = obs_own[0].reshape(round_count * row_count, model_width).astype(jnp.float32)
    own_normed = rms_norm(own_inputs, own_gain).astype(jnp.bfloat16)
    own_whole = lax.all_gather(weight_shard, "env", axis=0, tiled=True)
    own_state = own_inputs + jnp.dot(own_normed, own_whole, preferred_element_type=jnp.float32)
    every_pick = lax.all_gather(opponent_picks, "league", axis=0, tiled=True)
    action_range = jnp.arange(action_table.shape[0], dtype=jnp.int32)
    traj_list = []
    value_list = []
    for round_index in range(round_count):
        opp_raw = obs_opp[0, round_index].reshape(row_count, model_width)
        opp_inputs = opp_raw.astype(jnp.float32)
        all_rows = lax.all_gather(opp_raw, "league", axis=0, tiled=True)
        all_normed = rms_norm(all_rows.astype(jnp.float32), own_gain).astype(jnp.bfloat16)
        products = jnp.dot(all_normed, own_whole, preferred_element_type=jnp.float32)
        served = (every_pick[:, round_index] == my_group).astype(jnp.float32)
        products = (
            products.reshape(group_count, row_count, model_width) * served[:, None, None]
        ).reshape(group_count * row_count, model_width)
        opp_state = opp_inputs + lax.psum_scatter(
            products, "league", scatter_dimension=0, tiled=True
        )
        own_ids = actions[0, 0, round_index].reshape(row_count)
        opp_ids = actions[0, 1, round_index].reshape(row_count)
        onehot = (own_ids[:, None] == action_range[None, :]).astype(jnp.bfloat16) + (
            opp_ids[:, None] == action_range[None, :]
        ).astype(jnp.bfloat16)
        action_sum = jnp.dot(onehot, action_table, preferred_element_type=jnp.float32)
        round_state = lax.dynamic_slice_in_dim(own_state, round_index * row_count, row_count, 0)
        joint_sum = round_state + opp_state + action_sum
        joint_row = rms_norm(joint_sum, value_gain).astype(jnp.bfloat16)
        value_hidden = jax.nn.silu(
            jnp.dot(joint_row, value_up, preferred_element_type=jnp.float32)
        ).astype(jnp.bfloat16)
        value_est = jnp.dot(value_hidden, value_out, preferred_element_type=jnp.float32)
        value_list.append(value_est.reshape(env_count, step_count))
        time_block = joint_row.reshape(env_count, step_count, model_width).transpose(1, 2, 0)
        traj_list.append(lax.all_to_all(time_block, "env", split_axis=1, concat_axis=2, tiled=True))
    learner_rows = jnp.stack(traj_list)
    values = jnp.stack(value_list)
    return (learner_rows[None], values[None])


def solution(mesh):
    in_specs = (
        P("league", None, "env", None, None),
        P("league", None, "env", None, None),
        P("league", None, None, "env", None),
        P("league", None),
        P("league", "env", None),
        P("league", None),
        P(),
        P(),
        P(),
        P(),
    )
    out_specs = (P("league", None, None, "env", None), P("league", None, "env", None))
    return jax.shard_map(local, mesh=mesh, in_specs=in_specs, out_specs=out_specs, check_vma=False)
```

profile of v0, /device:TPU:0, one launch (start us, length us, event | category | flops | bytes accessed | tf_op | source)
XLA Modules:
  0.0 480.6 jit_solution(18280044370628031255)
XLA Ops:
  7.2 3.2 fusion.49
  10.5 0.7 all-gather.10.cloned.1.call-update
  11.3 0.7 all-gather.8.cloned.1.call-update
  12.0 6.0 %all-gather.1 = s32[4,1,2]{2,1,0:T(1,128)S(1)} all-gather(s32[1,1,2]{2,1,0:T(1,128)S(1)} %bitcast.98), channel_id=1, replica_groups=mesh['league'=4,'env'=8] {'league'}, dimensions={0}, use_global_device_ids=true | all-gather | bytes 40 | tf_op jit(solution)/shard_map/all_gather | solution.py:37
  18.0 0.1 copy.23
  18.2 29.6 %all-gather.6.cloned.1.call-done = bf16[1024,2048]{1,0:T(8,128)(2,1)} async-done(((bf16[256,2048]{1,0:T(8,128)(2,1)}), bf16[1024,2048]{1,0:T(8,128)(2,1)}) %all-gather.6.cloned.1.call-update) | async-done | bytes 4194320 | tf_op jit(solution)/shard_map/all_gather | solution.py:44
  47.8 3.1 fusion
  50.9 124.0 %all-gather.10.cloned.1.call-done = bf16[1,2048,2048]{2,1,0:T(8,128)(2,1)} async-done(((bf16[1,256,2048]{2,1,0:T(8,128)(2,1)}), bf16[1,2048,2048]{2,1,0:T(8,128)(2,1)}) %all-gather.10.cloned.1.call-update) | async-done | bytes 8388624 | tf_op jit(solution)/shard_map/all_gather | solution.py:35
  174.9 14.5 %fusion.12 = f32[1024,2048]{1,0:T(8,128)} fusion(bf16[1,2048,2048]{2,1,0:T(8,128)(2,1)} %all-gather.10.cloned.1.call-done, bf16[1024,2048]{1,0:T(8,128)(2,1)} %all-gather.6.cloned.1.call-done, f32[1024]{0:T(1024)S(1)} %bitcast.94, f32[2048]{0:T(1024)S(1)} %bitcast.90, f32[1024]{0:T(1024)S(1)} %add_rsqrt_fusion.2), kind=kOutput, calls=%fused_computation.16 | convolution fusion | flops 8600420352 | bytes 20987904 | tf_op jit(solution)/shard_map/dot_general | solution.py:46
  189.5 0.2 reduce-scatter.5.cloned.1.call-start
  189.7 19.5 %all-gather.8.cloned.1.call-done = bf16[1024,2048]{1,0:T(8,128)(2,1)} async-done(((bf16[256,2048]{1,0:T(8,128)(2,1)}), bf16[1024,2048]{1,0:T(8,128)(2,1)}) %all-gather.8.cloned.1.call-update) | async-done | bytes 4194320 | tf_op jit(solution)/shard_map/all_gather | solution.py:44
  209.2 3.2 fusion.3
  212.4 0.2 copy-done.6
  212.6 13.6 %fusion.15 = f32[1024,2048]{1,0:T(8,128)} fusion(bf16[1,2048,2048]{2,1,0:T(8,128)(2,1)} %all-gather.10.cloned.1.call-done, bf16[1024,2048]{1,0:T(8,128)(2,1)S(1)} %copy-done.6, f32[1024]{0:T(1024)S(1)} %bitcast.95, f32[1024]{0:T(1024)S(1)} %add_rsqrt_fusion.1, f32[2048]{0:T(1024)S(1)} %bitcast.91), kind=kOutput, calls=%fused_computation.17 | convolution fusion | flops 8600420352 | bytes 20987904 | tf_op jit(solution)/shard_map/dot_general | solution.py:46
  226.2 0.7 copy-done.9
  226.9 0.1 eq.86
  227.0 0.1 eq.82
  227.1 0.8 copy-done.4
  227.9 0.5 fusion.20
  228.4 0.1 rsqrt.44
  228.5 0.1 eq.95
  228.6 0.1 eq.91
  228.6 0.5 fusion.22
  229.2 1.0 copy-done.5
  230.2 9.6 %bitcast_add_fusion = f32[512,2048]{1,0:T(8,128)} fusion(bf16[1,2,16,16,2048]{4,3,2,1,0:T(8,128)(2,1)S(1)} %copy-done.5, bf16[512,2048]{1,0:T(8,128)(2,1)S(1)} %fusion.22, bf16[1,2048,2048]{2,1,0:T(8,128)(2,1)} %all-gather.10.cloned.1.call-done), kind=kOutput, calls=%fused_computation.18 | convolution fusion | flops 4297064448 | bytes 16777216 | tf_op jit(solution)/shard_map/dot_general | solution.py:36
  239.9 43.5 %reduce-scatter.3.cloned.1.call-done = f32[256,2048]{1,0:T(8,128)} async-done(((f32[1024,2048]{1,0:T(8,128)}), f32[256,2048]{1,0:T(8,128)}) %reduce-scatter.3.cloned.1.call-update) | async-done | bytes 2097168 | tf_op jit(solution)/shard_map/reduce_scatter | solution.py:51
  283.4 4.2 multiply_reduce_fusion.1
  287.6 70.1 %reduce-scatter.5.cloned.1.call-done = f32[256,2048]{1,0:T(8,128)} async-done(((f32[1024,2048]{1,0:T(8,128)}), f32[256,2048]{1,0:T(8,128)}) %reduce-scatter.5.cloned.1.call-update) | async-done | bytes 2097168 | tf_op jit(solution)/shard_map/reduce_scatter | solution.py:51
  357.7 3.1 multiply_reduce_fusion
  360.8 0.4 multiply_convert_fusion.1
  361.3 8.8 %copy.27 = bf16[16,16,2048]{0,1,2:T(8,128)(2,1)} copy(bf16[16,16,2048]{2,1,0:T(8,128)(2,1)S(1)} %bitcast.87) | data formatting | bytes 2097152 | tf_op jit(solution)/shard_map/reshape | solution.py:68
  370.1 7.5 %bitcast_bitcast_fusion = bf16[2048,16,16]{2,1,0:T(8,128)(2,1)} fusion(bf16[16,16,2048]{0,1,2:T(8,128)(2,1)} %copy.27), kind=kLoop, calls=%fused_computation.71 | loop fusion | bytes 2097152
  377.6 11.2 %reshape.107 = bf16[8,2,32768]{2,1,0:T(2,128)(2,1)} reshape(bf16[2048,16,16]{2,1,0:T(8,128)(2,1)} %bitcast_bitcast_fusion) | data formatting | bytes 2097152
  388.8 5.5 %all-to-all-start.1 = ((bf16[8,2,32768]{2,1,0:T(2,128)(2,1)}), bf16[8,2,32768]{2,1,0:T(2,128)(2,1)S(1)}, u32[]{:S(2)}, u32[]{:S(2)}) async-start(bf16[8,2,32768]{2,1,0:T(2,128)(2,1)} %reshape.107), calls=%async_computation.3 | async-start | bytes 2097152 | tf_op jit(solution)/shard_map/all_to_all | solution.py:69
  394.3 8.8 %copy.24 = bf16[16,16,2048]{0,1,2:T(8,128)(2,1)} copy(bf16[16,16,2048]{2,1,0:T(8,128)(2,1)S(1)} %bitcast.86) | data formatting | bytes 2097152 | tf_op jit(solution)/shard_map/reshape | solution.py:68
  403.1 7.5 %bitcast_bitcast_fusion.1 = bf16[2048,16,16]{2,1,0:T(8,128)(2,1)} fusion(bf16[16,16,2048]{0,1,2:T(8,128)(2,1)} %copy.24), kind=kLoop, calls=%fused_computation.72 | loop fusion | bytes 2097152
  410.6 11.2 %reshape.109 = bf16[8,2,32768]{2,1,0:T(2,128)(2,1)} reshape(bf16[2048,16,16]{2,1,0:T(8,128)(2,1)} %bitcast_bitcast_fusion.1) | data formatting | bytes 2097152
  421.8 6.0 %all-to-all-start = ((bf16[8,2,32768]{2,1,0:T(2,128)(2,1)}), bf16[8,2,32768]{2,1,0:T(2,128)(2,1)S(1)}, u32[]{:S(2)}, u32[]{:S(2)}) async-start(bf16[8,2,32768]{2,1,0:T(2,128)(2,1)} %reshape.109), calls=%async_computation.1 | async-start | bytes 2097152 | tf_op jit(solution)/shard_map/all_to_all | solution.py:69
  427.9 3.9 fusion.30
  431.8 0.1 stack_reshape.7
  431.9 4.0 fusion.29
  435.9 0.7 maximum_bitcast_fusion.1
  436.6 7.5 %reshape.108 = bf16[2048,16,16]{2,1,0:T(8,128)(2,1)} reshape(bf16[8,2,32768]{2,1,0:T(2,128)(2,1)S(1)} %all-to-all-done.1) | data formatting | bytes 2097152
  444.1 9.1 %copy.29 = bf16[16,256,8,16]{1,3,2,0:T(8,128)(2,1)} copy(bf16[16,256,8,16]{3,0,1,2:T(8,128)(2,1)} %bitcast.80) | data formatting | bytes 2097152 | tf_op jit(solution)/shard_map/all_to_all | solution.py:69
  453.3 7.5 %reshape.110 = bf16[2048,16,16]{2,1,0:T(8,128)(2,1)} reshape(bf16[8,2,32768]{2,1,0:T(2,128)(2,1)S(1)} %all-to-all-done) | data formatting | bytes 2097152
  460.8 9.1 %copy.26 = bf16[16,256,8,16]{1,3,2,0:T(8,128)(2,1)} copy(bf16[16,256,8,16]{3,0,1,2:T(8,128)(2,1)} %bitcast.81) | data formatting | bytes 2097152 | tf_op jit(solution)/shard_map/all_to_all | solution.py:69
  469.9 1.7 maximum_bitcast_fusion
  471.7 2.4 copy.30
  (47 shorter events, 0.5 us)
Async XLA Ops:
  7.2 276.2 %copy-start = (bf16[256,2048]{1,0:T(8,128)(2,1)S(1)}, bf16[256,2048]{1,0:T(8,128)(2,1)}, u32[]{:S(2)}) copy-start(bf16[256,2048]{1,0:T(8,128)(2,1)} %param.16) | copy-start | bytes 3145732
  7.2 4.8 %copy-start.13 = (s32[1,2]{1,0:T(1,128)S(1)}, s32[1,2]{1,0:T(1,128)}, u32[]{:S(2)}) copy-start(s32[1,2]{1,0:T(1,128)} %param.13) | copy-start | bytes 28
  7.2 11.0 %copy-start.10 = (bf16[1,2048]{1,0:T(2,128)(2,1)S(1)}, bf16[1,2048]{1,0:T(2,128)(2,1)}, u32[]{:S(2)}) copy-start(bf16[1,2048]{1,0:T(2,128)(2,1)} %param.15) | copy-start | bytes 12292
  7.2 40.6 %all-gather.6.cloned.1.call-start = ((), (), s32[]{:S(2)}) async-start(), calls=%async_computation.4 | async-start | bytes 5242880 | tf_op jit(solution)/shard_map/all_gather | solution.py:44
  10.5 164.4 %all-gather.10.cloned.1.call-start = ((), (), s32[]{:S(2)}) async-start(), calls=%async_computation.8 | async-start | bytes 9437184 | tf_op jit(solution)/shard_map/all_gather | solution.py:35
  11.2 197.9 %all-gather.8.cloned.1.call-start = ((), (), s32[]{:S(2)}) async-start(), calls=%async_computation.6 | async-start | bytes 5242880 | tf_op jit(solution)/shard_map/all_gather | solution.py:44
  12.0 271.4 %reduce-scatter.3.cloned.1.call-start = ((), (), s32[]{:S(2)}) async-start(), calls=%async_computation.5 | async-start | bytes 10485760 | tf_op jit(solution)/shard_map/reduce_scatter | solution.py:51
  189.5 168.2 %reduce-scatter.5.cloned.1.call-start = ((), (), s32[]{:S(2)}) async-start(), calls=%async_computation.7 | async-start | bytes 10485760 | tf_op jit(solution)/shard_map/reduce_scatter | solution.py:51
  209.2 3.4 copy-start.6
  226.2 0.8 copy-start.9
  226.2 1.7 copy-start.4
  226.2 2.3 copy-start.11
  228.6 1.6 copy-start.5
  230.2 53.1 %copy-start.2 = (bf16[1,1,16,16,2048]{4,3,2,1,0:T(8,128)(2,1)S(1)}, bf16[1,1,16,16,2048]{4,3,2,1,0:T(8,128)(2,1)}, u32[]{:S(2)}) copy-start(bf16[1,1,16,16,2048]{4,3,2,1,0:T(8,128)(2,1)} %get-tuple-element.8) | copy-start | bytes 3145732
  239.9 117.8 %copy-start.1 = (bf16[1,1,16,16,2048]{4,3,2,1,0:T(8,128)(2,1)S(1)}, bf16[1,1,16,16,2048]{4,3,2,1,0:T(8,128)(2,1)}, u32[]{:S(2)}) copy-start(bf16[1,1,16,16,2048]{4,3,2,1,0:T(8,128)(2,1)} %get-tuple-element.9) | copy-start | bytes 3145732
  357.7 3.1 copy-start.3
  361.2 8.8 %copy-start.8 = (bf16[256,2048]{1,0:T(8,128)(2,1)}, bf16[256,2048]{1,0:T(8,128)(2,1)S(1)}, u32[]{:S(2)}) copy-start(bf16[256,2048]{1,0:T(8,128)(2,1)S(1)} %get-tuple-element.15) | copy-start | bytes 3145732
  361.3 33.1 %copy-start.7 = (bf16[256,2048]{1,0:T(8,128)(2,1)}, bf16[256,2048]{1,0:T(8,128)(2,1)S(1)}, u32[]{:S(2)}) copy-start(bf16[256,2048]{1,0:T(8,128)(2,1)S(1)} %get-tuple-element.14) | copy-start | bytes 3145732
  388.8 33.0 %all-to-all-start.1 = ((bf16[8,2,32768]{2,1,0:T(2,128)(2,1)}), bf16[8,2,32768]{2,1,0:T(2,128)(2,1)S(1)}, u32[]{:S(2)}, u32[]{:S(2)}) async-start(bf16[8,2,32768]{2,1,0:T(2,128)(2,1)} %reshape.107), calls=%async_computation.3 | async-start | bytes 2097152 | tf_op jit(solution)/shard_map/all_to_all | solution.py:69
  410.6 17.2 %copy-start.12 = (bf16[1024]{0:T(1024)(128)(2,1)S(1)}, bf16[1024]{0:T(1024)(128)(2,1)}, u32[]{:S(2)}) copy-start(bf16[1024]{0:T(1024)(128)(2,1)} %param.19) | copy-start | bytes 6148
  421.8 31.4 %all-to-all-start = ((bf16[8,2,32768]{2,1,0:T(2,128)(2,1)}), bf16[8,2,32768]{2,1,0:T(2,128)(2,1)S(1)}, u32[]{:S(2)}, u32[]{:S(2)}) async-start(bf16[8,2,32768]{2,1,0:T(2,128)(2,1)} %reshape.109), calls=%async_computation.1 | async-start | bytes 2097152 | tf_op jit(solution)/shard_map/all_to_all | solution.py:69
Sparse Core Ops, SparseCore 0:
  10.6 37.1 all-gather.5
  49.9 124.9 all-gather.9
  176.5 32.6 all-gather.7
  211.6 71.7 reduce-scatter.2
  286.0 71.6 reduce-scatter.4
where the time goes:
time: 482 us; the launch traced here: 481 us
  waiting for transfers between devices  288 us (60%)
  local copies, waits for them, and re-layouts  97.5 us (20%)
  matrix products  52.9 us (11%)
  between operations  13.9 us (3%)
  starting transfers between devices  11.9 us (2%)
  other arithmetic  10.2 us (2%)
  blocking collectives  5.95 us (1%)
    all_gather x1, waiting for transfers between devices, local(): own_whole = lax.all_gather(weight_shard, 'env', axis=0, tiled=True)  124 us
    reduce_scatter x2, waiting for transfers between devices, local(): lax.psum_scatter(products, 'league', scatter_dimension=0, tiled=True)  114 us
    unnamed x39, local copies, waits for them, and re-layouts  57.8 us
    all_gather x2, waiting for transfers between devices, local(): all_rows = lax.all_gather(opp_raw, 'league', axis=0, tiled=True)  49.1 us
    dot_general x2, matrix products, local(): jnp.dot(all_normed, own_whole, preferred_element_type=jnp.float32)  28.1 us
    all_to_all x2, local copies, waits for them, and re-layouts, local(): lax.all_to_all(time_block, 'env', split_axis=1, concat_axis=2, tiled=True)  18.2 us
    reshape x2, local copies, waits for them, and re-layouts, local(): joint_row.reshape(env_count, step_count, model_width).transpose(1, 2, 0)  17.6 us
    all_to_all x2, starting transfers between devices, local(): lax.all_to_all(time_block, 'env', split_axis=1, concat_axis=2, tiled=True)  11.5 us
  transfers between devices with their start and end apart: 7, of which 5 were waited for; matrix products, arithmetic and copies ran while one was open for 21% of the time, Pallas kernels for 0%

commit v1 on v0

--- a/solution.py
+++ b/solution.py
@@ -32,7 +32,22 @@
     my_group = lax.axis_index("league")
     own_inputs = obs_own[0].reshape(round_count * row_count, model_width).astype(jnp.float32)
     own_normed = rms_norm(own_inputs, own_gain).astype(jnp.bfloat16)
-    own_whole = lax.all_gather(weight_shard, "env", axis=0, tiled=True)
+    ways, here, step = (lax.axis_size("env"), lax.axis_index("env"), weight_shard.shape[0])
+    shape = [n * ways if d == 0 else n for d, n in enumerate(weight_shard.shape)]
+    own_whole = lax.dynamic_update_slice_in_dim(
+        jnp.zeros(shape, weight_shard.dtype), weight_shard, here * step, axis=0
+    )
+    going_up = going_down = weight_shard
+    for far in range(1, ways // 2 + 1):
+        going_up = lax.ppermute(going_up, "env", [(d, (d + 1) % ways) for d in range(ways)])
+        own_whole = lax.dynamic_update_slice_in_dim(
+            own_whole, going_up, (here - far) % ways * step, axis=0
+        )
+        if 2 * far < ways:
+            going_down = lax.ppermute(going_down, "env", [(d, (d - 1) % ways) for d in range(ways)])
+            own_whole = lax.dynamic_update_slice_in_dim(
+                own_whole, going_down, (here + far) % ways * step, axis=0
+            )
     own_state = own_inputs + jnp.dot(own_normed, own_whole, preferred_element_type=jnp.float32)
     every_pick = lax.all_gather(opponent_picks, "league", axis=0, tiled=True)
     action_range = jnp.arange(action_table.shape[0], dtype=jnp.int32)

time: 482 us -> 467 us (0.969)
  waiting for transfers between devices: 288 us -> 236 us
  starting transfers between devices: 11.9 us -> 31.8 us
  local copies, waits for them, and re-layouts: 97.5 us -> 115 us
  other arithmetic: 10.2 us -> 16 us
  matrix products: 52.9 us -> 47.6 us
    ppermute x0 -> x7, waiting for transfers between devices: none -> 125 us  [the longest x4 125 us: local(): lax.ppermute(going_up, 'env', [(d, (d + 1) % ways) for d in range(ways)])]
    all_gather x1 -> x0, waiting for transfers between devices: 124 us -> none  [local(): own_whole = lax.all_gather(weight_shard, 'env', axis=0, tiled=True)]
    all_gather x2, waiting for transfers between devices: 49.1 us -> 0.02 us  [local(): all_rows = lax.all_gather(opp_raw, 'league', axis=0, tiled=True)]
    ppermute x0 -> x7, starting transfers between devices: none -> 20 us  [the longest x4 10.6 us: local(): lax.ppermute(going_up, 'env', [(d, (d + 1) % ways) for d in range(ways)])]
    dynamic_update_slice x0 -> x8, local copies, waits for them, and re-layouts: none -> 13.5 us  [the longest x4 8.06 us: local(): lax.dynamic_update_slice_in_dim(own_whole, going_up, (here - far) % ways...]
    reduce_sum x3 -> x4, other arithmetic: 6.75 us -> 12.5 us  [rms_norm(): scale = lax.rsqrt(jnp.mean(inputs * inputs, axis=-1, keepdims=True) + 1e-05)]
    unnamed x39 -> x41, local copies, waits for them, and re-layouts: 57.8 us -> 57.3 us
  transfers between devices with their start and end apart: 7 -> 13, of which waited for: 5 -> 7; matrix products, arithmetic and copies ran while one was open for 21% -> 25% of each run, Pallas kernels for 0% -> 0%
where the time goes in v1:
time: 467 us; the launch traced here: 466 us
  waiting for transfers between devices  236 us (51%)
  local copies, waits for them, and re-layouts  115 us (25%)
  matrix products  47.6 us (10%)
  starting transfers between devices  31.8 us (7%)
  other arithmetic  16 us (3%)
  between operations  14 us (3%)
  blocking collectives  5.03 us (1%)
    ppermute x4, waiting for transfers between devices, local(): lax.ppermute(going_up, 'env', [(d, (d + 1) % ways) for d in range(ways)])  125 us
    reduce_scatter x2, waiting for transfers between devices, local(): lax.psum_scatter(products, 'league', scatter_dimension=0, tiled=True)  111 us
    unnamed x41, local copies, waits for them, and re-layouts  57.3 us
    dot_general x2, matrix products, local(): jnp.dot(all_normed, own_whole, preferred_element_type=jnp.float32)  26.7 us
    all_to_all x2, local copies, waits for them, and re-layouts, local(): lax.all_to_all(time_block, 'env', split_axis=1, concat_axis=2, tiled=True)  18.2 us
    reshape x2, local copies, waits for them, and re-layouts, local(): joint_row.reshape(env_count, step_count, model_width).transpose(1, 2, 0)  17.6 us
    reduce_sum x4, other arithmetic, rms_norm(): scale = lax.rsqrt(jnp.mean(inputs * inputs, axis=-1, keepdims=True) + 1e-05)  12.5 us
    all_to_all x2, starting transfers between devices, local(): lax.all_to_all(time_block, 'env', split_axis=1, concat_axis=2, tiled=True)  11.5 us
  transfers between devices with their start and end apart: 13, of which 7 were waited for; matrix products, arithmetic and copies ran while one was open for 25% of the time, Pallas kernels for 0%

profile of v1, /device:TPU:0, one launch (start us, length us, event | category | flops | bytes accessed | tf_op | source)
XLA Modules:
  0.0 465.5 jit_solution(1026206039521137974)
XLA Ops:
  7.3 3.3 fusion.41
  10.7 3.0 collective-permute-start
  13.7 3.1 collective-permute-start.1
  16.9 41.7 %collective-permute-done = bf16[256,2048]{1,0:T(8,128)(2,1)} collective-permute-done((bf16[256,2048]{1,0:T(8,128)(2,1)S(1)}, bf16[256,2048]{1,0:T(8,128)(2,1)}, u32[]{:S(2)}, u32[]{:S(2)}) %collective-permute-start) | collective-permute-done | bytes 1048608 | tf_op jit(solution)/shard_map/ppermute | solution.py:42
  58.6 2.6 collective-permute-start.2
  61.2 3.0 collective-permute-start.3
  64.2 5.0 %all-gather = s32[4,1,2]{2,1,0:T(1,128)S(1)} all-gather(s32[1,1,2]{2,1,0:T(1,128)S(1)} %bitcast.94), channel_id=1, replica_groups=mesh['league'=4,'env'=8] {'league'}, dimensions={0}, use_global_device_ids=true | all-gather | bytes 40 | tf_op jit(solution)/shard_map/all_gather | solution.py:52
  69.3 36.2 %collective-permute-done.2 = bf16[256,2048]{1,0:T(8,128)(2,1)} collective-permute-done((bf16[256,2048]{1,0:T(8,128)(2,1)}, bf16[256,2048]{1,0:T(8,128)(2,1)}, u32[]{:S(2)}, u32[]{:S(2)}) %collective-permute-start.2) | collective-permute-done | bytes 1048608 | tf_op jit(solution)/shard_map/ppermute | solution.py:42
  105.5 2.5 collective-permute-start.4
  108.1 4.3 broadcast_in_dim.6
  112.4 1.1 constant_dynamic-update-slice_fusion.7
  113.5 3.2 collective-permute-start.5
  116.7 2.4 constant_dynamic-update-slice_fusion.6
  119.1 32.6 %collective-permute-done.4 = bf16[256,2048]{1,0:T(8,128)(2,1)} collective-permute-done((bf16[256,2048]{1,0:T(8,128)(2,1)}, bf16[256,2048]{1,0:T(8,128)(2,1)}, u32[]{:S(2)}, u32[]{:S(2)}) %collective-permute-start.4) | collective-permute-done | bytes 1048608 | tf_op jit(solution)/shard_map/ppermute | solution.py:42
  151.8 2.5 collective-permute-start.6
  154.3 1.0 constant_dynamic-update-slice_fusion.5
  155.3 2.3 constant_dynamic-update-slice_fusion.4
  157.6 2.3 constant_dynamic-update-slice_fusion.3
  159.9 2.3 constant_dynamic-update-slice_fusion.2
  163.3 14.3 %collective-permute-done.6 = bf16[256,2048]{1,0:T(8,128)(2,1)S(1)} collective-permute-done((bf16[256,2048]{1,0:T(8,128)(2,1)}, bf16[256,2048]{1,0:T(8,128)(2,1)S(1)}, u32[]{:S(2)}, u32[]{:S(2)}) %collective-permute-start.6) | collective-permute-done | bytes 1048608 | tf_op jit(solution)/shard_map/ppermute | solution.py:42
  177.6 1.1 constant_dynamic-update-slice_fusion
  178.6 3.2 fusion.3
  182.1 13.3 %convolution_multiply_fusion = f32[1024,2048]{1,0:T(8,128)} fusion(bf16[2048,2048]{1,0:T(8,128)(2,1)} %constant_dynamic-update-slice_fusion, bf16[1024,2048]{1,0:T(8,128)(2,1)S(1)} %copy-done.7, f32[1024]{0:T(1024)S(1)} %bitcast.90, f32[1024]{0:T(1024)S(1)} %add_rsqrt_fusion.1, f32[2048]{0:T(1024)S(1)} %bitcast.86), kind=kOutput, calls=%fused_computation.10 | convolution fusion | flops 8600420352 | bytes 20987904 | tf_op jit(solution)/shard_map/dot_general | solution.py:61
  195.7 3.2 fusion
  199.1 13.4 %convolution_multiply_fusion.1 = f32[1024,2048]{1,0:T(8,128)} fusion(bf16[2048,2048]{1,0:T(8,128)(2,1)} %constant_dynamic-update-slice_fusion, bf16[1024,2048]{1,0:T(8,128)(2,1)S(1)} %copy-done.6, f32[1024]{0:T(1024)S(1)} %bitcast.91, f32[2048]{0:T(1024)S(1)} %bitcast.87, f32[1024]{0:T(1024)S(1)} %add_rsqrt_fusion.2), kind=kOutput, calls=%fused_computation.11 | convolution fusion | flops 8600420352 | bytes 20987904 | tf_op jit(solution)/shard_map/dot_general | solution.py:61
  212.6 1.6 copy-done.4
  215.1 1.8 fusion.24
  216.9 1.8 fusion.28
  219.5 9.7 %bitcast_add_fusion = f32[512,2048]{1,0:T(8,128)} fusion(bf16[1,2,16,16,2048]{4,3,2,1,0:T(8,128)(2,1)S(1)} %copy-done.5, bf16[512,2048]{1,0:T(8,128)(2,1)S(1)} %fusion.10, bf16[2048,2048]{1,0:T(8,128)(2,1)} %constant_dynamic-update-slice_fusion), kind=kOutput, calls=%fused_computation.12 | convolution fusion | flops 4297064448 | bytes 16777216 | tf_op jit(solution)/shard_map/dot_general | solution.py:51
  229.2 36.6 %reduce-scatter.5.cloned.1.call-done = f32[256,2048]{1,0:T(8,128)} async-done(((f32[1024,2048]{1,0:T(8,128)}), f32[256,2048]{1,0:T(8,128)}) %reduce-scatter.5.cloned.1.call-update) | async-done | bytes 2097168 | tf_op jit(solution)/shard_map/reduce_scatter | solution.py:66
  265.7 74.4 %reduce-scatter.3.cloned.1.call-done = f32[256,2048]{1,0:T(8,128)} async-done(((f32[1024,2048]{1,0:T(8,128)}), f32[256,2048]{1,0:T(8,128)}) %reduce-scatter.3.cloned.1.call-update) | async-done | bytes 2097168 | tf_op jit(solution)/shard_map/reduce_scatter | solution.py:66
  340.1 5.6 %multiply_reduce_fusion.1 = (f32[256]{0:T(256)S(1)}, f32[256,2048]{1,0:T(8,128)S(1)}, f32[256]{0:T(256)S(1)}, f32[256,2048]{1,0:T(8,128)S(1)}) fusion(f32[256,2048]{1,0:T(8,128)} %fusion.28, f32[256,2048]{1,0:T(8,128)} %reduce-scatter.3.cloned.1.call-done, bf16[1,1,16,16,2048]{4,3,2,1,0:T(8,128)(2,1)S(1)} %copy-done.2, f32[512,2048]{1,0:T(8,128)} %bitcast_add_fusion, ...), kind=kLoop, calls=%fused_computation.30 | loop fusion | flops 6290944 | bytes 18876416 | tf_op jit(solution)/shard_map/reduce_sum | solution.py:8
  346.1 8.8 %copy.24 = bf16[16,16,2048]{0,1,2:T(8,128)(2,1)} copy(bf16[16,16,2048]{2,1,0:T(8,128)(2,1)S(1)} %bitcast.81) | data formatting | bytes 2097152 | tf_op jit(solution)/shard_map/reshape | solution.py:83
  354.9 7.5 %bitcast_bitcast_fusion.1 = bf16[2048,16,16]{2,1,0:T(8,128)(2,1)} fusion(bf16[16,16,2048]{0,1,2:T(8,128)(2,1)} %copy.24), kind=kLoop, calls=%fused_computation.76 | loop fusion | bytes 2097152
  362.4 11.2 %reshape.108 = bf16[8,2,32768]{2,1,0:T(2,128)(2,1)} reshape(bf16[2048,16,16]{2,1,0:T(8,128)(2,1)} %bitcast_bitcast_fusion.1) | data formatting | bytes 2097152
  373.7 5.5 %all-to-all-start = ((bf16[8,2,32768]{2,1,0:T(2,128)(2,1)}), bf16[8,2,32768]{2,1,0:T(2,128)(2,1)S(1)}, u32[]{:S(2)}, u32[]{:S(2)}) async-start(bf16[8,2,32768]{2,1,0:T(2,128)(2,1)} %reshape.108), calls=%async_computation.1 | async-start | bytes 2097152 | tf_op jit(solution)/shard_map/all_to_all | solution.py:84
  379.2 8.8 %copy.27 = bf16[16,16,2048]{0,1,2:T(8,128)(2,1)} copy(bf16[16,16,2048]{2,1,0:T(8,128)(2,1)S(1)} %bitcast.80) | data formatting | bytes 2097152 | tf_op jit(solution)/shard_map/reshape | solution.py:83
  388.0 7.5 %bitcast_bitcast_fusion = bf16[2048,16,16]{2,1,0:T(8,128)(2,1)} fusion(bf16[16,16,2048]{0,1,2:T(8,128)(2,1)} %copy.27), kind=kLoop, calls=%fused_computation.75 | loop fusion | bytes 2097152
  395.5 11.3 %reshape.106 = bf16[8,2,32768]{2,1,0:T(2,128)(2,1)} reshape(bf16[2048,16,16]{2,1,0:T(8,128)(2,1)} %bitcast_bitcast_fusion) | data formatting | bytes 2097152
  406.7 6.0 %all-to-all-start.1 = ((bf16[8,2,32768]{2,1,0:T(2,128)(2,1)}), bf16[8,2,32768]{2,1,0:T(2,128)(2,1)S(1)}, u32[]{:S(2)}, u32[]{:S(2)}) async-start(bf16[8,2,32768]{2,1,0:T(2,128)(2,1)} %reshape.106), calls=%async_computation.3 | async-start | bytes 2097152 | tf_op jit(solution)/shard_map/all_to_all | solution.py:84
  412.7 3.9 fusion.17
  416.7 3.7 fusion.18
  421.2 7.5 %reshape.109 = bf16[2048,16,16]{2,1,0:T(8,128)(2,1)} reshape(bf16[8,2,32768]{2,1,0:T(2,128)(2,1)S(1)} %all-to-all-done) | data formatting | bytes 2097152
  428.7 9.1 %copy.26 = bf16[16,256,8,16]{1,3,2,0:T(8,128)(2,1)} copy(bf16[16,256,8,16]{3,0,1,2:T(8,128)(2,1)} %bitcast.76) | data formatting | bytes 2097152 | tf_op jit(solution)/shard_map/all_to_all | solution.py:84
  438.1 7.5 %reshape.107 = bf16[2048,16,16]{2,1,0:T(8,128)(2,1)} reshape(bf16[8,2,32768]{2,1,0:T(2,128)(2,1)S(1)} %all-to-all-done.1) | data formatting | bytes 2097152
  445.7 9.1 %copy.29 = bf16[16,256,8,16]{1,3,2,0:T(8,128)(2,1)} copy(bf16[16,256,8,16]{3,0,1,2:T(8,128)(2,1)} %bitcast.77) | data formatting | bytes 2097152 | tf_op jit(solution)/shard_map/all_to_all | solution.py:84
  454.8 1.8 maximum_bitcast_fusion
  456.6 2.4 copy.30
  (70 shorter events, 5.4 us)
Async XLA Ops:
  7.2 207.9 %copy-start = (bf16[256,2048]{1,0:T(8,128)(2,1)S(1)}, bf16[256,2048]{1,0:T(8,128)(2,1)}, u32[]{:S(2)}) copy-start(bf16[256,2048]{1,0:T(8,128)(2,1)} %param.16) | copy-start | bytes 3145732
  7.2 3.5 copy-start.9
  7.2 57.0 %copy-start.14 = (s32[1,2]{1,0:T(1,128)S(1)}, s32[1,2]{1,0:T(1,128)}, u32[]{:S(2)}) copy-start(s32[1,2]{1,0:T(1,128)} %param.13) | copy-start | bytes 28
  7.2 100.9 %copy-start.11 = (bf16[1,2048]{1,0:T(2,128)(2,1)S(1)}, bf16[1,2048]{1,0:T(2,128)(2,1)}, u32[]{:S(2)}) copy-start(bf16[1,2048]{1,0:T(2,128)(2,1)} %param.15) | copy-start | bytes 12292
  7.2 171.4 %all-gather.6.cloned.1.call-start = ((), (), s32[]{:S(2)}) async-start(), calls=%async_computation.6 | async-start | bytes 5242880 | tf_op jit(solution)/shard_map/all_gather | solution.py:59
  10.6 185.1 %all-gather.4.cloned.1.call-start = ((), (), s32[]{:S(2)}) async-start(), calls=%async_computation.4 | async-start | bytes 5242880 | tf_op jit(solution)/shard_map/all_gather | solution.py:59
  10.7 47.9 %collective-permute-start = (bf16[256,2048]{1,0:T(8,128)(2,1)S(1)}, bf16[256,2048]{1,0:T(8,128)(2,1)}, u32[]{:S(2)}, u32[]{:S(2)}) collective-permute-start(bf16[256,2048]{1,0:T(8,128)(2,1)S(1)} %bitcast.84), channel_id=1, source_target_pairs={{0,1},{1,2},{2,3},{3,4},{4,5},{5,6},{6,7},{7,0},{8,9},{9,10},{10,1... | collective-permute-start | bytes 3145736 | tf_op jit(solution)/shard_map/ppermute | solution.py:42
  13.7 47.5 %collective-permute-start.1 = (bf16[256,2048]{1,0:T(8,128)(2,1)S(1)}, bf16[256,2048]{1,0:T(8,128)(2,1)S(1)}, u32[]{:S(2)}, u32[]{:S(2)}) collective-permute-start(bf16[256,2048]{1,0:T(8,128)(2,1)S(1)} %bitcast.85), channel_id=1, source_target_pairs={{0,7},{1,0},{2,1},{3,2},{4,3},{5,4},{6,5},{7,6},{8,15},{9,8},{10,9... | collective-permute-start | bytes 3145736 | tf_op jit(solution)/shard_map/ppermute | solution.py:47
  16.8 248.9 %reduce-scatter.5.cloned.1.call-start = ((), (), s32[]{:S(2)}) async-start(), calls=%async_computation.7 | async-start | bytes 10485760 | tf_op jit(solution)/shard_map/reduce_scatter | solution.py:66
  58.6 46.9 %collective-permute-start.2 = (bf16[256,2048]{1,0:T(8,128)(2,1)}, bf16[256,2048]{1,0:T(8,128)(2,1)}, u32[]{:S(2)}, u32[]{:S(2)}) collective-permute-start(bf16[256,2048]{1,0:T(8,128)(2,1)} %collective-permute-done), channel_id=1, source_target_pairs={{0,1},{1,2},{2,3},{3,4},{4,5},{5,6},{6,7},{7,0},{8,9},{9,10},{10,1... | collective-permute-start | bytes 3145736 | tf_op jit(solution)/shard_map/ppermute | solution.py:42
  61.2 52.3 %collective-permute-start.3 = (bf16[256,2048]{1,0:T(8,128)(2,1)S(1)}, bf16[256,2048]{1,0:T(8,128)(2,1)}, u32[]{:S(2)}, u32[]{:S(2)}) collective-permute-start(bf16[256,2048]{1,0:T(8,128)(2,1)S(1)} %collective-permute-done.1), channel_id=1, source_target_pairs={{0,7},{1,0},{2,1},{3,2},{4,3},{5,4},{6,5},{7,6},{8,15},{9,8},{10,9... | collective-permute-start | bytes 3145736 | tf_op jit(solution)/shard_map/ppermute | solution.py:47
  105.5 46.3 %collective-permute-start.4 = (bf16[256,2048]{1,0:T(8,128)(2,1)}, bf16[256,2048]{1,0:T(8,128)(2,1)}, u32[]{:S(2)}, u32[]{:S(2)}) collective-permute-start(bf16[256,2048]{1,0:T(8,128)(2,1)} %collective-permute-done.2), channel_id=1, source_target_pairs={{0,1},{1,2},{2,3},{3,4},{4,5},{5,6},{6,7},{7,0},{8,9},{9,10},{10,1... | collective-permute-start | bytes 3145736 | tf_op jit(solution)/shard_map/ppermute | solution.py:42
  113.5 48.7 %collective-permute-start.5 = (bf16[256,2048]{1,0:T(8,128)(2,1)}, bf16[256,2048]{1,0:T(8,128)(2,1)S(1)}, u32[]{:S(2)}, u32[]{:S(2)}) collective-permute-start(bf16[256,2048]{1,0:T(8,128)(2,1)} %collective-permute-done.3), channel_id=1, source_target_pairs={{0,7},{1,0},{2,1},{3,2},{4,3},{5,4},{6,5},{7,6},{8,15},{9,8},{10,9... | collective-permute-start | bytes 3145736 | tf_op jit(solution)/shard_map/ppermute | solution.py:47
  151.8 25.8 %collective-permute-start.6 = (bf16[256,2048]{1,0:T(8,128)(2,1)}, bf16[256,2048]{1,0:T(8,128)(2,1)S(1)}, u32[]{:S(2)}, u32[]{:S(2)}) collective-permute-start(bf16[256,2048]{1,0:T(8,128)(2,1)} %collective-permute-done.4), channel_id=1, source_target_pairs={{0,1},{1,2},{2,3},{3,4},{4,5},{5,6},{6,7},{7,0},{8,9},{9,10},{10,1... | collective-permute-start | bytes 3145736 | tf_op jit(solution)/shard_map/ppermute | solution.py:42
  178.6 3.4 copy-start.7
  195.4 144.7 %reduce-scatter.3.cloned.1.call-start = ((), (), s32[]{:S(2)}) async-start(), calls=%async_computation.5 | async-start | bytes 10485760 | tf_op jit(solution)/shard_map/reduce_scatter | solution.py:66
  195.7 3.5 copy-start.6
  212.5 1.6 copy-start.4
  212.5 2.2 copy-start.10
  212.5 2.5 copy-start.12
  216.9 2.6 copy-start.5
  219.5 120.6 %copy-start.2 = (bf16[1,1,16,16,2048]{4,3,2,1,0:T(8,128)(2,1)S(1)}, bf16[1,1,16,16,2048]{4,3,2,1,0:T(8,128)(2,1)}, u32[]{:S(2)}) copy-start(bf16[1,1,16,16,2048]{4,3,2,1,0:T(8,128)(2,1)} %get-tuple-element.14) | copy-start | bytes 3145732
  219.5 120.6 %copy-start.3 = (bf16[1,1,16,16,2048]{4,3,2,1,0:T(8,128)(2,1)S(1)}, bf16[1,1,16,16,2048]{4,3,2,1,0:T(8,128)(2,1)}, u32[]{:S(2)}) copy-start(bf16[1,1,16,16,2048]{4,3,2,1,0:T(8,128)(2,1)} %get-tuple-element.15) | copy-start | bytes 3145732
  346.1 8.8 %copy-start.8 = (bf16[256,2048]{1,0:T(8,128)(2,1)}, bf16[256,2048]{1,0:T(8,128)(2,1)S(1)}, u32[]{:S(2)}) copy-start(bf16[256,2048]{1,0:T(8,128)(2,1)S(1)} %get-tuple-element.20) | copy-start | bytes 3145732
  373.7 33.1 %all-to-all-start = ((bf16[8,2,32768]{2,1,0:T(2,128)(2,1)}), bf16[8,2,32768]{2,1,0:T(2,128)(2,1)S(1)}, u32[]{:S(2)}, u32[]{:S(2)}) async-start(bf16[8,2,32768]{2,1,0:T(2,128)(2,1)} %reshape.108), calls=%async_computation.1 | async-start | bytes 2097152 | tf_op jit(solution)/shard_map/all_to_all | solution.py:84
  395.5 17.3 %copy-start.13 = (bf16[1024]{0:T(1024)(128)(2,1)S(1)}, bf16[1024]{0:T(1024)(128)(2,1)}, u32[]{:S(2)}) copy-start(bf16[1024]{0:T(1024)(128)(2,1)} %param.19) | copy-start | bytes 6148
  406.7 31.4 %all-to-all-start.1 = ((bf16[8,2,32768]{2,1,0:T(2,128)(2,1)}), bf16[8,2,32768]{2,1,0:T(2,128)(2,1)S(1)}, u32[]{:S(2)}, u32[]{:S(2)}) async-start(bf16[8,2,32768]{2,1,0:T(2,128)(2,1)} %reshape.106), calls=%async_computation.3 | async-start | bytes 2097152 | tf_op jit(solution)/shard_map/all_to_all | solution.py:84
  454.8 4.2 copy-start.1
Sparse Core Ops, SparseCore 0:
  10.7 37.1 all-gather.5
  49.5 34.4 all-gather.3
  195.5 70.1 reduce-scatter.4
  268.3 71.7 reduce-scatter.2
